TPU v7x, 32 devices: a whole 2x2x4 slice. The times are simulated.
32 devices in a mesh: row: 8 (over z, core), col: 4 (over y, x).
Axes of the slice: x: 2, y: 2, z: 4, core: 2. Of those that a mesh axis runs over, the one named last changes fastest.
Arguments:
- tokens: bfloat16 [16384, 1024], P(('row', 'col')), may hold values from -64 to 64, as said below
- merge_map: int32 [16384], P(('row', 'col')), may hold values from 0 to 511, as said below
- block_owner: int32 [32, 8], P(('row', 'col')), may hold values from -1 to 15, as said below
- neighbours: int32 [64, 4], P(('row', 'col')), may hold values from 0 to 7, as said below
- w_query: bfloat16 [1024, 512], replicated, may hold values from -0.1875 to 0.1875
- w_key: bfloat16 [1024, 512], replicated, may hold values from -0.1875 to 0.1875
- w_value: bfloat16 [1024, 512], replicated, may hold values from -0.1875 to 0.1875
Outputs:
- attended: bfloat16 [16384, 512], P(('row', 'col'))
Inputs may be any that keep to these rules, and one draw needn't show every extreme that they name: `merge_map`: within a tile, the slots of its live blocks (those whose block_owner is not -1) are each used by one or more tokens, and no other slot is used. `block_owner`: A tile's live blocks are its first ones, 1 to 8 of them, 8 in some tile of every column index; a code o names owned block o % 2 of the device with row index o // 2 and the tile's column index; within one column index every code is named exactly once; one tile names each row index at most once. `neighbours`: the entries of a row are distinct, and the first is the block's own candidate number. `tokens`: finite bfloat16 values.
All inputs are finite; a program needn't handle non-finite values.
Results may differ from a plain program's by a relative error of at most 0.019.
The roundings to bfloat16 on the way count: a program that leaves them out, or rounds other values in their place, can miss the bound.
Values may be sent and summed in bfloat16 or wider, within the bound.
No kernel may reach another device: no remote copies, remote signals or barrier semaphores. Data moves between devices by JAX's collectives and lax.ppermute only.
A program may use at most 64 MiB of HBM per device.

v0:
```python
import functools
import math

import jax
import jax.numpy as jnp
from jax import lax
from jax.experimental import pallas as pl
from jax.experimental.pallas import tpu as pltpu
from jax.sharding import PartitionSpec as P


HD = 64
BLK = 64
OWN = 2
LANES = 128
TAG = 8


VMEM = pl.BlockSpec(memory_space=pltpu.VMEM)
SMEM = pl.BlockSpec(memory_space=pltpu.SMEM)
HBM = pl.BlockSpec(memory_space=pltpu.HBM)
PARAMS = pltpu.CompilerParams(vmem_limit_bytes=16 << 20)


def partner(i, k, n, back=False):
    if n & (n - 1) == 0:
        return i ^ k
    return (i - k + n) % n if back else (i + k) % n


def inner(i, k, n, back=False):
    m = n // 2
    side = (i >= m) * m
    return side + partner(i - side, k, m, back)


def across(i, n):
    m = n // 2
    return i + m - (i >= m) * n


def peer(i, k, n, back=False):
    m = n // 2
    return inner(i, k, n, back) if k < m else across(inner(i, k - m, n, back), n)


def order(n):
    return sorted(range(1, n), key=lambda k: (-(k.bit_length() - 1 if k > 1 else 0), k))


def rounds(x, axis, n, to):
    out = list(x)
    for k in order(len(x)):
        out[k] = lax.ppermute(x[k], axis, [(i, to(i, k, n)) for i in range(n)])
    return out


def cost(us):
    return pl.CostEstimate(
        flops=int(us * 8e8), bytes_accessed=int(us * 2e6), transcendentals=0
    )


FIRST = (0, BLK // 2)
SECOND = (BLK // 2, BLK - BLK // 2)
PARTS = (FIRST, SECOND)
MESSAGES = (
    ((True, *FIRST),),
    ((True, *SECOND), (False, *FIRST)),
    ((False, *SECOND),),
)


def slot_of(owner_ref, row, slots):
    slot = jnp.int32(-1)
    code = jnp.int32(-1)
    for b in range(slots):
        o = owner_ref[0, b]
        hit = (o >= 0) & (o // OWN == row)
        slot = jnp.where(hit, b, slot)
        code = jnp.where(hit, o % OWN, code)
    return slot, code


def merge_kernel(n, slots, messages, tok_hbm, map_hbm, owner_hbm, *refs):
    m = n // 2
    outs = refs[: m * len(messages)]
    tok_ref, map_ref, owner_ref, sems = refs[m * len(messages) :]
    copies = [
        pltpu.make_async_copy(src, dst, sems.at[i])
        for i, (src, dst) in enumerate(
            [(owner_hbm, owner_ref), (map_hbm, map_ref), (tok_hbm, tok_ref)]
        )
    ]
    for copy in copies:
        copy.start()
    me = lax.axis_index("row")
    toks, width = tok_ref.shape
    pieces = width // LANES
    copies[0].wait()
    dest = {}
    for far in sorted({part[0] for message in messages for part in message}):
        for k in range(m):
            to = inner(me, k, n)
            dest[far, k] = slot_of(owner_ref, across(to, n) if far else to, slots)
    work = []
    for i, message in enumerate(messages):
        at = 0
        for far, start, rows in message:
            work += [(i * m + k, at, dest[far, k], start, rows) for k in range(m)]
            at += rows * pieces
            if start == 0:
                end = sum(part[2] for part in message) * pieces
                for k in range(m):
                    outs[i * m + k][end:, :] = jnp.full(
                        (TAG, LANES), dest[far, k][1], jnp.int32
                    ).astype(jnp.bfloat16)
    copies[1].wait()
    mm = map_ref[...]
    waited = False
    while work:
        group, total = [], 0
        while work and total + work[0][4] <= 256:
            group.append(work.pop(0))
            total += group[-1][4]
        hot = []
        for _, _, (slot, _), start, rows in group:
            base = jnp.where(slot >= 0, slot * BLK + start, -BLK)
            line = lax.broadcasted_iota(jnp.int32, (rows, toks), 0)
            hot.append(mm == line + base)
        hot = jnp.concatenate(hot, axis=0).astype(jnp.float32)
        scale = 1.0 / jnp.maximum(jnp.sum(hot, axis=1, keepdims=True), 1.0)
        if not waited:
            copies[2].wait()
            waited = True
        sums = jnp.dot(hot.astype(jnp.bfloat16), tok_ref[...], preferred_element_type=jnp.float32)
        merged = (sums * scale).astype(jnp.bfloat16)
        row = 0
        for out, at, _, _, rows in group:
            for h in range(pieces):
                outs[out][at + h * rows : at + (h + 1) * rows, :] = merged[
                    row : row + rows, h * LANES : (h + 1) * LANES
                ]
            row += rows


def pad(m):
    return -(-m // TAG) * TAG


def is_slot(tag, s):
    return tag[0:1, :].astype(jnp.float32) == float(s)


def masks_of(tags, rows):
    return [[jnp.broadcast_to(is_slot(tag, s), (rows, LANES)) for s in range(OWN)] for tag in tags]


def gather_kernel(m, rows, tagged, *refs):
    blocks = refs[:m]
    if tagged:
        (out_ref,) = refs[m:]
        size = out_ref.shape[0] - pad(m)
        for k in range(m):
            out_ref[size + k : size + k + 1, :] = blocks[k][size // OWN : size // OWN + 1, :]
        tags = [blocks[k][size // OWN : size // OWN + TAG, :] for k in range(m)]
    else:
        known_ref, out_ref = refs[m:]
        size = out_ref.shape[0]
        first = known_ref.shape[0] - pad(m)
        tags = [known_ref[first + k : first + k + 1, :] for k in range(m)]
    masks = masks_of(tags, rows)
    for h in range(0, size // OWN, rows):
        pick = [jnp.zeros((rows, LANES), jnp.bfloat16)] * OWN
        for k in range(m):
            block = blocks[k][h : h + rows, :]
            pick = [jnp.where(masks[k][s], block, pick[s]) for s in range(OWN)]
        for s in range(OWN):
            out_ref[s * (size // OWN) + h : s * (size // OWN) + h + rows, :] = pick[s]


def project_kernel(m, rows, tagged, skip, wq_ref, wk_ref, wv_ref, cross_ref, *refs):
    blocks, refs = refs[:m], refs[m:]
    if tagged:
        q_ref, kv_ref, tag_ref, x_ref = refs
    else:
        tag_ref, q_ref, kv_ref, x_ref = refs
    pieces = x_ref.shape[1] // LANES
    size = pieces * rows
    if tagged:
        for k in range(m):
            tag_ref[k] = blocks[k][skip + size : skip + size + TAG, :]
            tag_ref[m + k] = jnp.broadcast_to(
                cross_ref[OWN * size + k : OWN * size + k + 1, :], (TAG, LANES)
            )
    masks = masks_of([tag_ref[k] for k in range(m)], rows)
    for h in range(pieces):
        pick = [jnp.zeros((rows, LANES), jnp.bfloat16)] * OWN
        for k in range(m):
            block = blocks[k][skip + h * rows : skip + (h + 1) * rows, :]
            pick = [jnp.where(masks[k][s], block, pick[s]) for s in range(OWN)]
        for s in range(OWN):
            other = cross_ref[s * size + h * rows : s * size + (h + 1) * rows, :]
            x_ref[s * rows : (s + 1) * rows, h * LANES : (h + 1) * LANES] = pick[s] + other
    x = x_ref[...]
    width = wk_ref.shape[1]

    def mul(w):
        return jnp.dot(x, w[...], preferred_element_type=jnp.float32).astype(jnp.bfloat16)

    kv_ref[:, :width] = mul(wk_ref)
    kv_ref[:, width:] = mul(wv_ref)
    q_ref[...] = mul(wq_ref)


def attend_kernel(n, n_col, near_ref, tag_ref, *refs):
    my_col = lax.axis_index("col")
    chunks = PARTS
    near = near_ref.shape[1]
    refs = list(refs)
    qs, refs = refs[: len(chunks)], refs[len(chunks) :]
    kvs, refs = refs[: len(chunks) * n_col], refs[len(chunks) * n_col :]
    outs, (kv_ref, head_ref) = refs[:n], refs[n:]
    width = qs[0].shape[1]
    for s in range(OWN):
        place = jnp.int32(0)
        for k in range(n_col):
            col = partner(my_col, k, n_col, True)
            for t in range(OWN):
                cand = col * OWN + t
                hit = near_ref[s, 0] == cand
                for j in range(1, near):
                    hit = hit | (near_ref[s, j] == cand)

                @pl.when(hit)
                def _(place=place):
                    for c, (start, rows) in enumerate(chunks):
                        at = pl.multiple_of(place * BLK + start, 8)
                        kv_ref[s, pl.ds(at, rows), :] = kvs[c * n_col + k][
                            t * rows : (t + 1) * rows, :
                        ]

                place = place + jnp.where(hit, 1, 0)
    scale = 1.0 / math.sqrt(HD)
    low = lax.broadcasted_iota(jnp.int32, (BLK, LANES), 1) < HD
    zero = jnp.zeros((BLK, LANES), jnp.bfloat16)
    for s in range(OWN):
        for h in range(0, width, LANES):
            q = jnp.concatenate(
                [
                    qs[c][s * rows : (s + 1) * rows, h : h + LANES]
                    for c, (_, rows) in enumerate(chunks)
                ],
                axis=0,
            )
            q = jnp.concatenate([jnp.where(low, q, zero), jnp.where(low, zero, q)], axis=0)
            score = lax.dot_general(
                q,
                kv_ref[s, :, h : h + LANES],
                (((1,), (1,)), ((), ())),
                preferred_element_type=jnp.float32,
            )
            score = score * scale
            p = jnp.exp(score - jnp.max(score, axis=1, keepdims=True))
            total = jnp.sum(p, axis=1, keepdims=True)
            o = jnp.dot(
                p.astype(jnp.bfloat16),
                kv_ref[s, :, width + h : width + h + LANES],
                preferred_element_type=jnp.float32,
            )
            o = (o * (1.0 / total)).astype(jnp.bfloat16)
            head_ref[s, :, h : h + LANES] = jnp.where(low, o[:BLK], o[BLK:])
    for k in range(n):
        masks = [
            jnp.broadcast_to(is_slot(tag_ref[k], s), (BLK, LANES)) for s in range(OWN)
        ]
        for h in range(0, width, LANES):
            pick = zero
            for s in range(OWN):
                pick = jnp.where(masks[s], head_ref[s, :, h : h + LANES], pick)
            outs[k][:, h : h + LANES] = pick


def spread_kernel(n, slots, map_ref, owner_ref, out_ref):
    me = lax.axis_index("row")
    mm = map_ref[...]
    block = mm // BLK
    target = mm % BLK
    for k in range(n):
        slot, _ = slot_of(owner_ref, peer(me, k, n), slots)
        target = target + jnp.where((block == slot) & (slot >= 0), k * BLK, 0)
    toks = mm.shape[1]
    for k0 in range(0, n * BLK, LANES):
        ids = lax.broadcasted_iota(jnp.int32, (LANES, toks), 0) + k0
        hot = (ids == target).astype(jnp.float32)
        out_ref[:, k0 : k0 + LANES] = jnp.transpose(hot).astype(jnp.bfloat16)


def return_kernel(n, spread_ref, *refs):
    blocks, out_ref, all_ref = refs[:n], refs[n], refs[n + 1]
    for k in range(n):
        all_ref[k * BLK : (k + 1) * BLK, :] = blocks[k][...]
    out_ref[...] = jnp.dot(
        spread_ref[...], all_ref[...], preferred_element_type=jnp.float32
    ).astype(out_ref.dtype)


def on_device(tokens, merge_map, block_owner, neighbours, w_query, w_key, w_value):
    n = lax.axis_size("row")
    n_col = lax.axis_size("col")
    toks, width = tokens.shape
    heads = w_query.shape[1]
    slots = block_owner.shape[1]
    near = neighbours.shape[1]
    bf16 = jnp.bfloat16

    def shape(*s, dtype=bf16):
        return jax.ShapeDtypeStruct(s, dtype)

    mm = pltpu.with_memory_space_constraint(merge_map.reshape(1, toks), pltpu.HBM)
    tokens = pltpu.with_memory_space_constraint(tokens, pltpu.HBM)
    block_owner = pltpu.with_memory_space_constraint(block_owner, pltpu.HBM)
    neighbours = pltpu.with_memory_space_constraint(neighbours, pltpu.HBM)
    m = n // 2
    pieces = width // LANES

    def merge(*which):
        messages = tuple(MESSAGES[i] for i in which)
        shapes = []
        for message in messages:
            size = sum(part[2] for part in message) * pieces
            size += TAG * any(part[1] == 0 for part in message)
            shapes += [shape(size, LANES)] * m
        outs = pl.pallas_call(
            functools.partial(merge_kernel, n, slots, messages),
            out_shape=shapes,
            in_specs=[HBM] * 3,
            out_specs=[VMEM] * len(shapes),
            scratch_shapes=[
                pltpu.VMEM((toks, width), bf16),
                pltpu.VMEM((1, toks), jnp.int32),
                pltpu.SMEM(block_owner.shape, jnp.int32),
                pltpu.SemaphoreType.DMA((3,)),
            ],
            compiler_params=PARAMS,
            cost_estimate=cost(2),
            name="merge",
        )(tokens, mm, block_owner)
        return [outs[i * m : (i + 1) * m] for i in range(len(which))]

    def gather(c, blocks, *known):
        rows = PARTS[c][1]
        out = pl.pallas_call(
            functools.partial(gather_kernel, m, rows, not known),
            out_shape=shape(OWN * rows * pieces + (0 if known else pad(m)), LANES),
            in_specs=[VMEM] * (m + len(known)),
            out_specs=VMEM,
            compiler_params=PARAMS,
            cost_estimate=cost(0.5),
            name="gather",
        )(*blocks, *known)
        return out, lax.ppermute(out, "row", [(i, across(i, n)) for i in range(n)])

    def project(c, skip, cross, blocks, *tags):
        rows = PARTS[c][1]
        out = pl.pallas_call(
            functools.partial(project_kernel, m, rows, not tags, skip),
            out_shape=[shape(OWN * rows, heads), shape(OWN * rows, 2 * heads)]
            + [shape(n, TAG, LANES)] * (not tags),
            in_specs=[VMEM] * (4 + m + len(tags)),
            out_specs=[VMEM] * (2 + (not tags)),
            scratch_shapes=[pltpu.VMEM((OWN * rows, width), bf16)],
            compiler_params=PARAMS,
            cost_estimate=cost(1),
            name="project",
        )(w_query, w_key, w_value, cross, *blocks, *tags)
        return out, rounds([out[1]] * n_col, "col", n_col, partner)

    (far0,) = merge(0)
    far0 = rounds(far0, "row", n, inner)
    far1, home1 = merge(1, 2)
    far1 = rounds(far1, "row", n, inner)
    known, cross0 = gather(0, far0)
    home1 = rounds(home1, "row", n, inner)
    _, cross1 = gather(1, far1, known)
    (q0, _, tags), kv0 = project(0, SECOND[1] * pieces, cross0, far1)
    (q1, _), kv1 = project(1, 0, cross1, home1, tags)
    qs, kvs = [q0, q1], kv0 + kv1
    spread = pl.pallas_call(
        functools.partial(spread_kernel, n, slots),
        out_shape=shape(toks, n * BLK),
        in_specs=[VMEM, SMEM],
        out_specs=VMEM,
        compiler_params=PARAMS,
        cost_estimate=cost(2),
        name="spread",
    )(mm, block_owner)
    replies = pl.pallas_call(
        functools.partial(attend_kernel, n, n_col),
        out_shape=[shape(BLK, heads)] * n,
        in_specs=[SMEM] + [VMEM] * (1 + len(qs) + len(kvs)),
        out_specs=[VMEM] * n,
        scratch_shapes=[
            pltpu.VMEM((OWN, near * BLK, 2 * heads), bf16),
            pltpu.VMEM((OWN, BLK, heads), bf16),
        ],
        compiler_params=PARAMS,
        cost_estimate=cost(3),
        name="attend",
    )(neighbours, tags, *qs, *kvs)
    returned = rounds(replies, "row", n, functools.partial(peer, back=True))
    return pl.pallas_call(
        functools.partial(return_kernel, n),
        out_shape=shape(toks, heads),
        in_specs=[VMEM] * (1 + n),
        out_specs=VMEM,
        scratch_shapes=[pltpu.VMEM((n * BLK, heads), bf16)],
        compiler_params=PARAMS,
        cost_estimate=cost(2),
        name="give_back",
    )(spread, *returned)


def solution(mesh):
    in_specs = (
        P(("row", "col"), None),
        P(("row", "col")),
        P(("row", "col"), None),
        P(("row", "col"), None),
        P(),
        P(),
        P(),
    )
    out_specs = P(("row", "col"), None)

    return jax.shard_map(
        on_device, mesh=mesh, in_specs=in_specs, out_specs=out_specs, check_vma=False
    )
```

profile of v0, /device:TPU:13, one launch (start us, length us, event | category | flops | bytes accessed | tf_op | source)
XLA Modules:
  0.0 56.3 jit_solution(6202519031052405022)
XLA Ops:
  0.0 1.6 %merge.2 = (bf16[264,128]{1,0:T(8,128)(2,1)S(1)}, bf16[264,128]{1,0:T(8,128)(2,1)S(1)}, bf16[264,128]{1,0:T(8,128)(2,1)S(1)}, bf16[264,128]{1,0:T(8,128)(2,1)S(1)}) custom-call(bf16[512,1024]{1,0:T(8,128)(2,1)} %tok_hbm.3, s32[1,512]{1,0:T(1,128)} %bitcast.1, s32[1,8]{1,0:T(1,128)} %owner_hbm.3), custom_call_target="tpu_custom_call" | custom-call | flops 1600000000 | bytes 4000000 | tf_op jit(solution)/shard_map/merge/pallas_call | solution.py:334
  1.6 0.7 %collective-permute-start = (bf16[264,128]{1,0:T(8,128)(2,1)S(1)}, bf16[264,128]{1,0:T(8,128)(2,1)S(1)}, u32[]{:S(2)}, u32[]{:S(2)}) collective-permute-start(bf16[264,128]{1,0:T(8,128)(2,1)S(1)} %get-tuple-element.31), channel_id=1, source_target_pairs={{0,4},{4,0},{8,12},{12,8},{16,20},{20,16},{24,28},{28,24},{1,5},{5... | collective-permute-start | bytes 202760 | tf_op jit(solution)/shard_map/ppermute | solution.py:54
  2.5 1.5 %collective-permute-start.2 = (bf16[264,128]{1,0:T(8,128)(2,1)S(1)}, bf16[264,128]{1,0:T(8,128)(2,1)S(1)}, u32[]{:S(2)}, u32[]{:S(2)}) collective-permute-start(bf16[264,128]{1,0:T(8,128)(2,1)S(1)} %get-tuple-element.33), channel_id=1, source_target_pairs={{0,12},{4,8},{8,4},{12,0},{16,28},{20,24},{24,20},{28,16},{1,13},{... | collective-permute-start | bytes 202760 | tf_op jit(solution)/shard_map/ppermute | solution.py:54
  4.0 1.9 %merge.3 = (bf16[520,128]{1,0:T(8,128)(2,1)S(1)}, bf16[520,128]{1,0:T(8,128)(2,1)S(1)}, bf16[520,128]{1,0:T(8,128)(2,1)S(1)}, bf16[520,128]{1,0:T(8,128)(2,1)S(1...) custom-call(bf16[512,1024]{1,0:T(8,128)(2,1)} %tok_hbm.3, ...), custom_call_target="tpu_custom_call" | custom-call | flops 1600000000 | bytes 4000000 | tf_op jit(solution)/shard_map/merge/pallas_call | solution.py:334
  6.4 1.8 %collective-permute-start.6 = (bf16[520,128]{1,0:T(8,128)(2,1)S(1)}, bf16[520,128]{1,0:T(8,128)(2,1)S(1)}, u32[]{:S(2)}, u32[]{:S(2)}) collective-permute-start(bf16[520,128]{1,0:T(8,128)(2,1)S(1)} %get-tuple-element.37), channel_id=1, source_target_pairs={{0,12},{4,8},{8,4},{12,0},{16,28},{20,24},{24,20},{28,16},{1,13},{... | collective-permute-start | bytes 399368 | tf_op jit(solution)/shard_map/ppermute | solution.py:54
  8.3 2.4 %collective-permute-start.3 = (bf16[520,128]{1,0:T(8,128)(2,1)S(1)}, bf16[520,128]{1,0:T(8,128)(2,1)S(1)}, u32[]{:S(2)}, u32[]{:S(2)}) collective-permute-start(bf16[520,128]{1,0:T(8,128)(2,1)S(1)} %gather.2.refs_4_), channel_id=1, source_target_pairs={{0,16},{4,20},{8,24},{12,28},{16,0},{20,4},{24,8},{28,12},{1,17},{... | collective-permute-start | bytes 399368 | tf_op jit(solution)/shard_map/ppermute | solution.py:362
  11.2 1.3 %collective-permute-start.9 = (bf16[256,128]{1,0:T(8,128)(2,1)S(1)}, bf16[256,128]{1,0:T(8,128)(2,1)S(1)}, u32[]{:S(2)}, u32[]{:S(2)}) collective-permute-start(bf16[256,128]{1,0:T(8,128)(2,1)S(1)} %get-tuple-element.42), channel_id=1, source_target_pairs={{0,8},{4,12},{8,0},{12,4},{16,24},{20,28},{24,16},{28,20},{1,9},{5... | collective-permute-start | bytes 196616 | tf_op jit(solution)/shard_map/ppermute | solution.py:54
  12.5 2.6 %collective-permute-done.6.refs_3_ = bf16[520,128]{1,0:T(8,128)(2,1)S(1)} collective-permute-done((bf16[520,128]{1,0:T(8,128)(2,1)S(1)}, bf16[520,128]{1,0:T(8,128)(2,1)S(1)}, u32[]{:S(2)}, u32[]{:S(2)}) %collective-permute-start.6) | collective-permute-done | bytes 133152 | tf_op jit(solution)/shard_map/ppermute | solution.py:54
  15.2 5.3 %collective-permute-start.7 = (bf16[512,128]{1,0:T(8,128)(2,1)S(1)}, bf16[512,128]{1,0:T(8,128)(2,1)S(1)}, u32[]{:S(2)}, u32[]{:S(2)}) collective-permute-start(bf16[512,128]{1,0:T(8,128)(2,1)S(1)} %gather.3), channel_id=1, source_target_pairs={{0,16},{4,20},{8,24},{12,28},{16,0},{20,4},{24,8},{28,12},{1,17},{... | collective-permute-start | bytes 393224 | tf_op jit(solution)/shard_map/ppermute | solution.py:362
  20.5 0.7 %project.2 = (bf16[64,512]{1,0:T(8,128)(2,1)S(1)}, bf16[64,1024]{1,0:T(8,128)(2,1)S(1)}, bf16[8,8,128]{2,1,0:T(8,128)(2,1)S(1)}) custom-call(bf16[1024,512]{1,0:T(8,128)(2,1)S(1)} %copy-done, bf16[1024,512]{1,0:T(8,128)(2,1)S(1)} %copy-done.1, bf16[1024,512]{1,0:T(8,128)(2,1)S(1)} %copy-done.2, bf16[520,128]{1,0:T(8,128)(2,1)S(1)} %collective-permute-done.3.cross_ref, ...), custom_call_target="tpu_custom_call" | custom-call | flops 800000000 | bytes 2000000 | tf_op jit(solution)/shard_map/project/pallas_call | solution.py:366
  21.2 1.3 %collective-permute-start.11 = (bf16[64,1024]{1,0:T(8,128)(2,1)S(1)}, bf16[64,1024]{1,0:T(8,128)(2,1)S(1)}, u32[]{:S(2)}, u32[]{:S(2)}) collective-permute-start(bf16[64,1024]{1,0:T(8,128)(2,1)S(1)} %get-tuple-element.45.refs_2_), channel_id=1, source_target_pairs={{0,1},{1,0},{2,3},{3,2},{4,5},{5,4},{6,7},{7,6},{8,9},{9,8},{10,11... | collective-permute-start | bytes 393224 | tf_op jit(solution)/shard_map/ppermute | solution.py:54
  22.7 1.2 %collective-permute-start.13 = (bf16[64,1024]{1,0:T(8,128)(2,1)S(1)}, bf16[64,1024]{1,0:T(8,128)(2,1)S(1)}, u32[]{:S(2)}, u32[]{:S(2)}) collective-permute-start(bf16[64,1024]{1,0:T(8,128)(2,1)S(1)} %get-tuple-element.45.refs_2_), channel_id=1, source_target_pairs={{0,3},{1,2},{2,1},{3,0},{4,7},{5,6},{6,5},{7,4},{8,11},{9,10},{10,... | collective-permute-start | bytes 393224 | tf_op jit(solution)/shard_map/ppermute | solution.py:54
  23.9 1.0 %collective-permute-done.7.cross_ref = bf16[512,128]{1,0:T(8,128)(2,1)S(1)} collective-permute-done((bf16[512,128]{1,0:T(8,128)(2,1)S(1)}, bf16[512,128]{1,0:T(8,128)(2,1)S(1)}, u32[]{:S(2)}, u32[]{:S(2)}) %collective-permute-start.7) | collective-permute-done | bytes 131104 | tf_op jit(solution)/shard_map/ppermute | solution.py:362
  24.9 0.7 %project.3 = (bf16[64,512]{1,0:T(8,128)(2,1)S(1)}, bf16[64,1024]{1,0:T(8,128)(2,1)S(1)}) custom-call(bf16[1024,512]{1,0:T(8,128)(2,1)S(1)} %copy-done, bf16[1024,512]{1,0:T(8,128)(2,1)S(1)} %copy-done.1, bf16[1024,512]{1,0:T(8,128)(2,1)S(1)} %copy-done.2, bf16[512,128]{1,0:T(8,128)(2,1)S(1)} %collective-permute-done.7.cross_ref, ...), custom_call_target="tpu_custom_call" | custom-call | flops 800000000 | bytes 2000000 | tf_op jit(solution)/shard_map/project/pallas_call | solution.py:366
  25.6 1.3 %collective-permute-start.14 = (bf16[64,1024]{1,0:T(8,128)(2,1)S(1)}, bf16[64,1024]{1,0:T(8,128)(2,1)S(1)}, u32[]{:S(2)}, u32[]{:S(2)}) collective-permute-start(bf16[64,1024]{1,0:T(8,128)(2,1)S(1)} %get-tuple-element.46.refs_6_), channel_id=1, source_target_pairs={{0,1},{1,0},{2,3},{3,2},{4,5},{5,4},{6,7},{7,6},{8,9},{9,8},{10,11... | collective-permute-start | bytes 393224 | tf_op jit(solution)/shard_map/ppermute | solution.py:54
  27.1 1.2 %collective-permute-start.16 = (bf16[64,1024]{1,0:T(8,128)(2,1)S(1)}, bf16[64,1024]{1,0:T(8,128)(2,1)S(1)}, u32[]{:S(2)}, u32[]{:S(2)}) collective-permute-start(bf16[64,1024]{1,0:T(8,128)(2,1)S(1)} %get-tuple-element.46.refs_6_), channel_id=1, source_target_pairs={{0,3},{1,2},{2,1},{3,0},{4,7},{5,6},{6,5},{7,4},{8,11},{9,10},{10,... | collective-permute-start | bytes 393224 | tf_op jit(solution)/shard_map/ppermute | solution.py:54
  28.3 2.5 %collective-permute-done.12.refs_4_ = bf16[64,1024]{1,0:T(8,128)(2,1)S(1)} collective-permute-done((bf16[64,1024]{1,0:T(8,128)(2,1)S(1)}, bf16[64,1024]{1,0:T(8,128)(2,1)S(1)}, u32[]{:S(2)}, u32[]{:S(2)}) %collective-permute-start.12) | collective-permute-done | bytes 131104 | tf_op jit(solution)/shard_map/ppermute | solution.py:54
  30.8 1.1 %collective-permute-done.14.refs_7_ = bf16[64,1024]{1,0:T(8,128)(2,1)S(1)} collective-permute-done((bf16[64,1024]{1,0:T(8,128)(2,1)S(1)}, bf16[64,1024]{1,0:T(8,128)(2,1)S(1)}, u32[]{:S(2)}, u32[]{:S(2)}) %collective-permute-start.14) | collective-permute-done | bytes 131104 | tf_op jit(solution)/shard_map/ppermute | solution.py:54
  32.0 4.3 %collective-permute-done.15.refs_8_ = bf16[64,1024]{1,0:T(8,128)(2,1)S(1)} collective-permute-done((bf16[64,1024]{1,0:T(8,128)(2,1)S(1)}, bf16[64,1024]{1,0:T(8,128)(2,1)S(1)}, u32[]{:S(2)}, u32[]{:S(2)}) %collective-permute-start.15) | collective-permute-done | bytes 131104 | tf_op jit(solution)/shard_map/ppermute | solution.py:54
  36.3 1.8 %attend.1 = (bf16[64,512]{1,0:T(8,128)(2,1)S(1)}, bf16[64,512]{1,0:T(8,128)(2,1)S(1)}, bf16[64,512]{1,0:T(8,128)(2,1)S(1)}, bf16[64,512]{1,0:T(8,128)(2,1)S(1)},...) custom-call(s32[2,4]{1,0:T(2,128)} %near_ref.1, ...), custom_call_target="tpu_custom_call" | custom-call | flops 2400000000 | bytes 6000000 | tf_op jit(solution)/shard_map/attend/pallas_call | solution.py:398
  38.1 0.5 collective-permute-start.17
  38.6 1.4 %collective-permute-start.18 = (bf16[64,512]{1,0:T(8,128)(2,1)S(1)}, bf16[64,512]{1,0:T(8,128)(2,1)S(1)}, u32[]{:S(2)}, u32[]{:S(2)}) collective-permute-start(bf16[64,512]{1,0:T(8,128)(2,1)S(1)} %get-tuple-element.49), channel_id=1, source_target_pairs={{0,8},{4,12},{8,0},{12,4},{16,24},{20,28},{24,16},{28,20},{1,9},{5... | collective-permute-start | bytes 196616 | tf_op jit(solution)/shard_map/ppermute | solution.py:54
  40.4 2.0 %collective-permute-start.20 = (bf16[64,512]{1,0:T(8,128)(2,1)S(1)}, bf16[64,512]{1,0:T(8,128)(2,1)S(1)}, u32[]{:S(2)}, u32[]{:S(2)}) collective-permute-start(bf16[64,512]{1,0:T(8,128)(2,1)S(1)} %get-tuple-element.51), channel_id=1, source_target_pairs={{0,16},{4,20},{8,24},{12,28},{16,0},{20,4},{24,8},{28,12},{1,17},{... | collective-permute-start | bytes 196616 | tf_op jit(solution)/shard_map/ppermute | solution.py:54
  42.3 0.7 %collective-permute-start.21 = (bf16[64,512]{1,0:T(8,128)(2,1)S(1)}, bf16[64,512]{1,0:T(8,128)(2,1)S(1)}, u32[]{:S(2)}, u32[]{:S(2)}) collective-permute-start(bf16[64,512]{1,0:T(8,128)(2,1)S(1)} %get-tuple-element.52), channel_id=1, source_target_pairs={{0,20},{4,16},{8,28},{12,24},{16,4},{20,0},{24,12},{28,8},{1,21},{... | collective-permute-start | bytes 196616 | tf_op jit(solution)/shard_map/ppermute | solution.py:54
  43.0 0.8 %collective-permute-start.22 = (bf16[64,512]{1,0:T(8,128)(2,1)S(1)}, bf16[64,512]{1,0:T(8,128)(2,1)S(1)}, u32[]{:S(2)}, u32[]{:S(2)}) collective-permute-start(bf16[64,512]{1,0:T(8,128)(2,1)S(1)} %get-tuple-element.53), channel_id=1, source_target_pairs={{0,24},{4,28},{8,16},{12,20},{16,8},{20,12},{24,0},{28,4},{1,25},{... | collective-permute-start | bytes 196616 | tf_op jit(solution)/shard_map/ppermute | solution.py:54
  43.8 0.9 %collective-permute-start.23 = (bf16[64,512]{1,0:T(8,128)(2,1)S(1)}, bf16[64,512]{1,0:T(8,128)(2,1)S(1)}, u32[]{:S(2)}, u32[]{:S(2)}) collective-permute-start(bf16[64,512]{1,0:T(8,128)(2,1)S(1)} %get-tuple-element.54), channel_id=1, source_target_pairs={{0,28},{4,24},{8,20},{12,16},{16,12},{20,8},{24,4},{28,0},{1,29},{... | collective-permute-start | bytes 196616 | tf_op jit(solution)/shard_map/ppermute | solution.py:54
  44.8 1.1 %spread.1.spread_ref = bf16[512,512]{1,0:T(8,128)(2,1)S(1)} custom-call(s32[1,512]{1,0:T(1,128)} %bitcast.3, s32[1,8]{1,0:T(1,128)} %owner_hbm.3), custom_call_target="tpu_custom_call" | custom-call | flops 1600000000 | bytes 4000000 | tf_op jit(solution)/shard_map/spread/pallas_call | solution.py:389
  45.9 0.6 %collective-permute-done.20.refs_4_ = bf16[64,512]{1,0:T(8,128)(2,1)S(1)} collective-permute-done((bf16[64,512]{1,0:T(8,128)(2,1)S(1)}, bf16[64,512]{1,0:T(8,128)(2,1)S(1)}, u32[]{:S(2)}, u32[]{:S(2)}) %collective-permute-start.20) | collective-permute-done | bytes 65568 | tf_op jit(solution)/shard_map/ppermute | solution.py:54
  46.5 4.4 %collective-permute-done.21.refs_5_ = bf16[64,512]{1,0:T(8,128)(2,1)S(1)} collective-permute-done((bf16[64,512]{1,0:T(8,128)(2,1)S(1)}, bf16[64,512]{1,0:T(8,128)(2,1)S(1)}, u32[]{:S(2)}, u32[]{:S(2)}) %collective-permute-start.21) | collective-permute-done | bytes 65568 | tf_op jit(solution)/shard_map/ppermute | solution.py:54
  50.9 2.6 %collective-permute-done.22.refs_6_ = bf16[64,512]{1,0:T(8,128)(2,1)S(1)} collective-permute-done((bf16[64,512]{1,0:T(8,128)(2,1)S(1)}, bf16[64,512]{1,0:T(8,128)(2,1)S(1)}, u32[]{:S(2)}, u32[]{:S(2)}) %collective-permute-start.22) | collective-permute-done | bytes 65568 | tf_op jit(solution)/shard_map/ppermute | solution.py:54
  53.4 1.7 %collective-permute-done.23.refs_7_ = bf16[64,512]{1,0:T(8,128)(2,1)S(1)} collective-permute-done((bf16[64,512]{1,0:T(8,128)(2,1)S(1)}, bf16[64,512]{1,0:T(8,128)(2,1)S(1)}, u32[]{:S(2)}, u32[]{:S(2)}) %collective-permute-start.23) | collective-permute-done | bytes 65568 | tf_op jit(solution)/shard_map/ppermute | solution.py:54
  55.1 1.2 %give_back.1 = bf16[512,512]{1,0:T(8,128)(2,1)} custom-call(bf16[512,512]{1,0:T(8,128)(2,1)S(1)} %spread.1.spread_ref, bf16[64,512]{1,0:T(8,128)(2,1)S(1)} %get-tuple-element.47.refs_0_, bf16[64,512]{1,0:T(8,128)(2,1)S(1)} %collective-permute-done.17.refs_1_, bf16[64,512]{1,0:T(8,128)(2,1)S(1)} %collective-permute-done.18.refs_2_, ...), custom_call_target="tpu_custom_call" | custom-call | flops 1600000000 | bytes 4000000 | tf_op jit(solution)/shard_map/give_back/pallas_call | solution.py:412
  (31 shorter events, 2.1 us)
Async XLA Ops:
  1.6 4.8 %collective-permute-start = (bf16[264,128]{1,0:T(8,128)(2,1)S(1)}, bf16[264,128]{1,0:T(8,128)(2,1)S(1)}, u32[]{:S(2)}, u32[]{:S(2)}) collective-permute-start(bf16[264,128]{1,0:T(8,128)(2,1)S(1)} %get-tuple-element.31), channel_id=1, source_target_pairs={{0,4},{4,0},{8,12},{12,8},{16,20},{20,16},{24,28},{28,24},{1,5},{5... | collective-permute-start | bytes 202760 | tf_op jit(solution)/shard_map/ppermute | solution.py:54
  2.3 5.9 %collective-permute-start.1 = (bf16[264,128]{1,0:T(8,128)(2,1)S(1)}, bf16[264,128]{1,0:T(8,128)(2,1)S(1)}, u32[]{:S(2)}, u32[]{:S(2)}) collective-permute-start(bf16[264,128]{1,0:T(8,128)(2,1)S(1)} %get-tuple-element.32), channel_id=1, source_target_pairs={{0,8},{4,12},{8,0},{12,4},{16,24},{20,28},{24,16},{28,20},{1,9},{5... | collective-permute-start | bytes 202760 | tf_op jit(solution)/shard_map/ppermute | solution.py:54
  2.5 5.7 %collective-permute-start.2 = (bf16[264,128]{1,0:T(8,128)(2,1)S(1)}, bf16[264,128]{1,0:T(8,128)(2,1)S(1)}, u32[]{:S(2)}, u32[]{:S(2)}) collective-permute-start(bf16[264,128]{1,0:T(8,128)(2,1)S(1)} %get-tuple-element.33), channel_id=1, source_target_pairs={{0,12},{4,8},{8,4},{12,0},{16,28},{20,24},{24,20},{28,16},{1,13},{... | collective-permute-start | bytes 202760 | tf_op jit(solution)/shard_map/ppermute | solution.py:54
  4.0 16.5 %copy-start.2 = (bf16[1024,512]{1,0:T(8,128)(2,1)S(1)}, bf16[1024,512]{1,0:T(8,128)(2,1)}, u32[]{:S(2)}) copy-start(bf16[1024,512]{1,0:T(8,128)(2,1)} %wv_ref.3) | copy-start | bytes 3145732
  6.0 5.0 %collective-permute-start.4 = (bf16[520,128]{1,0:T(8,128)(2,1)S(1)}, bf16[520,128]{1,0:T(8,128)(2,1)S(1)}, u32[]{:S(2)}, u32[]{:S(2)}) collective-permute-start(bf16[520,128]{1,0:T(8,128)(2,1)S(1)} %get-tuple-element.35), channel_id=1, source_target_pairs={{0,4},{4,0},{8,12},{12,8},{16,20},{20,16},{24,28},{28,24},{1,5},{5... | collective-permute-start | bytes 399368 | tf_op jit(solution)/shard_map/ppermute | solution.py:54
  6.2 5.0 %collective-permute-start.5 = (bf16[520,128]{1,0:T(8,128)(2,1)S(1)}, bf16[520,128]{1,0:T(8,128)(2,1)S(1)}, u32[]{:S(2)}, u32[]{:S(2)}) collective-permute-start(bf16[520,128]{1,0:T(8,128)(2,1)S(1)} %get-tuple-element.36), channel_id=1, source_target_pairs={{0,8},{4,12},{8,0},{12,4},{16,24},{20,28},{24,16},{28,20},{1,9},{5... | collective-permute-start | bytes 399368 | tf_op jit(solution)/shard_map/ppermute | solution.py:54
  6.4 8.8 %collective-permute-start.6 = (bf16[520,128]{1,0:T(8,128)(2,1)S(1)}, bf16[520,128]{1,0:T(8,128)(2,1)S(1)}, u32[]{:S(2)}, u32[]{:S(2)}) collective-permute-start(bf16[520,128]{1,0:T(8,128)(2,1)S(1)} %get-tuple-element.37), channel_id=1, source_target_pairs={{0,12},{4,8},{8,4},{12,0},{16,28},{20,24},{24,20},{28,16},{1,13},{... | collective-permute-start | bytes 399368 | tf_op jit(solution)/shard_map/ppermute | solution.py:54
  8.2 12.3 %copy-start.1 = (bf16[1024,512]{1,0:T(8,128)(2,1)S(1)}, bf16[1024,512]{1,0:T(8,128)(2,1)}, u32[]{:S(2)}) copy-start(bf16[1024,512]{1,0:T(8,128)(2,1)} %wk_ref.3) | copy-start | bytes 3145732
  8.3 12.2 %copy-start = (bf16[1024,512]{1,0:T(8,128)(2,1)S(1)}, bf16[1024,512]{1,0:T(8,128)(2,1)}, u32[]{:S(2)}) copy-start(bf16[1024,512]{1,0:T(8,128)(2,1)} %wq_ref.3) | copy-start | bytes 3145732
  8.3 12.2 %collective-permute-start.3 = (bf16[520,128]{1,0:T(8,128)(2,1)S(1)}, bf16[520,128]{1,0:T(8,128)(2,1)S(1)}, u32[]{:S(2)}, u32[]{:S(2)}) collective-permute-start(bf16[520,128]{1,0:T(8,128)(2,1)S(1)} %gather.2.refs_4_), channel_id=1, source_target_pairs={{0,16},{4,20},{8,24},{12,28},{16,0},{20,4},{24,8},{28,12},{1,17},{... | collective-permute-start | bytes 399368 | tf_op jit(solution)/shard_map/ppermute | solution.py:362
  10.7 11.8 %collective-permute-start.10 = (bf16[256,128]{1,0:T(8,128)(2,1)S(1)}, bf16[256,128]{1,0:T(8,128)(2,1)S(1)}, u32[]{:S(2)}, u32[]{:S(2)}) collective-permute-start(bf16[256,128]{1,0:T(8,128)(2,1)S(1)} %get-tuple-element.43), channel_id=1, source_target_pairs={{0,12},{4,8},{8,4},{12,0},{16,28},{20,24},{24,20},{28,16},{1,13},{... | collective-permute-start | bytes 196616 | tf_op jit(solution)/shard_map/ppermute | solution.py:54
  11.0 11.7 %collective-permute-start.8 = (bf16[256,128]{1,0:T(8,128)(2,1)S(1)}, bf16[256,128]{1,0:T(8,128)(2,1)S(1)}, u32[]{:S(2)}, u32[]{:S(2)}) collective-permute-start(bf16[256,128]{1,0:T(8,128)(2,1)S(1)} %get-tuple-element.41), channel_id=1, source_target_pairs={{0,4},{4,0},{8,12},{12,8},{16,20},{20,16},{24,28},{28,24},{1,5},{5... | collective-permute-start | bytes 196616 | tf_op jit(solution)/shard_map/ppermute | solution.py:54
  11.2 12.7 %collective-permute-start.9 = (bf16[256,128]{1,0:T(8,128)(2,1)S(1)}, bf16[256,128]{1,0:T(8,128)(2,1)S(1)}, u32[]{:S(2)}, u32[]{:S(2)}) collective-permute-start(bf16[256,128]{1,0:T(8,128)(2,1)S(1)} %get-tuple-element.42), channel_id=1, source_target_pairs={{0,8},{4,12},{8,0},{12,4},{16,24},{20,28},{24,16},{28,20},{1,9},{5... | collective-permute-start | bytes 196616 | tf_op jit(solution)/shard_map/ppermute | solution.py:54
  15.2 9.7 %collective-permute-start.7 = (bf16[512,128]{1,0:T(8,128)(2,1)S(1)}, bf16[512,128]{1,0:T(8,128)(2,1)S(1)}, u32[]{:S(2)}, u32[]{:S(2)}) collective-permute-start(bf16[512,128]{1,0:T(8,128)(2,1)S(1)} %gather.3), channel_id=1, source_target_pairs={{0,16},{4,20},{8,24},{12,28},{16,0},{20,4},{24,8},{28,12},{1,17},{... | collective-permute-start | bytes 393224 | tf_op jit(solution)/shard_map/ppermute | solution.py:362
  21.2 5.9 %collective-permute-start.11 = (bf16[64,1024]{1,0:T(8,128)(2,1)S(1)}, bf16[64,1024]{1,0:T(8,128)(2,1)S(1)}, u32[]{:S(2)}, u32[]{:S(2)}) collective-permute-start(bf16[64,1024]{1,0:T(8,128)(2,1)S(1)} %get-tuple-element.45.refs_2_), channel_id=1, source_target_pairs={{0,1},{1,0},{2,3},{3,2},{4,5},{5,4},{6,7},{7,6},{8,9},{9,8},{10,11... | collective-permute-start | bytes 393224 | tf_op jit(solution)/shard_map/ppermute | solution.py:54
  22.5 8.3 %collective-permute-start.12 = (bf16[64,1024]{1,0:T(8,128)(2,1)S(1)}, bf16[64,1024]{1,0:T(8,128)(2,1)S(1)}, u32[]{:S(2)}, u32[]{:S(2)}) collective-permute-start(bf16[64,1024]{1,0:T(8,128)(2,1)S(1)} %get-tuple-element.45.refs_2_), channel_id=1, source_target_pairs={{0,2},{1,3},{2,0},{3,1},{4,6},{5,7},{6,4},{7,5},{8,10},{9,11},{10,... | collective-permute-start | bytes 393224 | tf_op jit(solution)/shard_map/ppermute | solution.py:54
  22.7 8.1 %collective-permute-start.13 = (bf16[64,1024]{1,0:T(8,128)(2,1)S(1)}, bf16[64,1024]{1,0:T(8,128)(2,1)S(1)}, u32[]{:S(2)}, u32[]{:S(2)}) collective-permute-start(bf16[64,1024]{1,0:T(8,128)(2,1)S(1)} %get-tuple-element.45.refs_2_), channel_id=1, source_target_pairs={{0,3},{1,2},{2,1},{3,0},{4,7},{5,6},{6,5},{7,4},{8,11},{9,10},{10,... | collective-permute-start | bytes 393224 | tf_op jit(solution)/shard_map/ppermute | solution.py:54
  25.6 6.3 %collective-permute-start.14 = (bf16[64,1024]{1,0:T(8,128)(2,1)S(1)}, bf16[64,1024]{1,0:T(8,128)(2,1)S(1)}, u32[]{:S(2)}, u32[]{:S(2)}) collective-permute-start(bf16[64,1024]{1,0:T(8,128)(2,1)S(1)} %get-tuple-element.46.refs_6_), channel_id=1, source_target_pairs={{0,1},{1,0},{2,3},{3,2},{4,5},{5,4},{6,7},{7,6},{8,9},{9,8},{10,11... | collective-permute-start | bytes 393224 | tf_op jit(solution)/shard_map/ppermute | solution.py:54
  26.9 9.4 %collective-permute-start.15 = (bf16[64,1024]{1,0:T(8,128)(2,1)S(1)}, bf16[64,1024]{1,0:T(8,128)(2,1)S(1)}, u32[]{:S(2)}, u32[]{:S(2)}) collective-permute-start(bf16[64,1024]{1,0:T(8,128)(2,1)S(1)} %get-tuple-element.46.refs_6_), channel_id=1, source_target_pairs={{0,2},{1,3},{2,0},{3,1},{4,6},{5,7},{6,4},{7,5},{8,10},{9,11},{10,... | collective-permute-start | bytes 393224 | tf_op jit(solution)/shard_map/ppermute | solution.py:54
  27.1 9.2 %collective-permute-start.16 = (bf16[64,1024]{1,0:T(8,128)(2,1)S(1)}, bf16[64,1024]{1,0:T(8,128)(2,1)S(1)}, u32[]{:S(2)}, u32[]{:S(2)}) collective-permute-start(bf16[64,1024]{1,0:T(8,128)(2,1)S(1)} %get-tuple-element.46.refs_6_), channel_id=1, source_target_pairs={{0,3},{1,2},{2,1},{3,0},{4,7},{5,6},{6,5},{7,4},{8,11},{9,10},{10,... | collective-permute-start | bytes 393224 | tf_op jit(solution)/shard_map/ppermute | solution.py:54
  38.1 4.9 %collective-permute-start.17 = (bf16[64,512]{1,0:T(8,128)(2,1)S(1)}, bf16[64,512]{1,0:T(8,128)(2,1)S(1)}, u32[]{:S(2)}, u32[]{:S(2)}) collective-permute-start(bf16[64,512]{1,0:T(8,128)(2,1)S(1)} %get-tuple-element.48), channel_id=1, source_target_pairs={{0,4},{4,0},{8,12},{12,8},{16,20},{20,16},{24,28},{28,24},{1,5},{5... | collective-permute-start | bytes 196616 | tf_op jit(solution)/shard_map/ppermute | solution.py:54
  38.6 5.2 %collective-permute-start.18 = (bf16[64,512]{1,0:T(8,128)(2,1)S(1)}, bf16[64,512]{1,0:T(8,128)(2,1)S(1)}, u32[]{:S(2)}, u32[]{:S(2)}) collective-permute-start(bf16[64,512]{1,0:T(8,128)(2,1)S(1)} %get-tuple-element.49), channel_id=1, source_target_pairs={{0,8},{4,12},{8,0},{12,4},{16,24},{20,28},{24,16},{28,20},{1,9},{5... | collective-permute-start | bytes 196616 | tf_op jit(solution)/shard_map/ppermute | solution.py:54
  40.0 5.9 %collective-permute-start.19 = (bf16[64,512]{1,0:T(8,128)(2,1)S(1)}, bf16[64,512]{1,0:T(8,128)(2,1)S(1)}, u32[]{:S(2)}, u32[]{:S(2)}) collective-permute-start(bf16[64,512]{1,0:T(8,128)(2,1)S(1)} %get-tuple-element.50), channel_id=1, source_target_pairs={{0,12},{4,8},{8,4},{12,0},{16,28},{20,24},{24,20},{28,16},{1,13},{... | collective-permute-start | bytes 196616 | tf_op jit(solution)/shard_map/ppermute | solution.py:54
  40.4 6.2 %collective-permute-start.20 = (bf16[64,512]{1,0:T(8,128)(2,1)S(1)}, bf16[64,512]{1,0:T(8,128)(2,1)S(1)}, u32[]{:S(2)}, u32[]{:S(2)}) collective-permute-start(bf16[64,512]{1,0:T(8,128)(2,1)S(1)} %get-tuple-element.51), channel_id=1, source_target_pairs={{0,16},{4,20},{8,24},{12,28},{16,0},{20,4},{24,8},{28,12},{1,17},{... | collective-permute-start | bytes 196616 | tf_op jit(solution)/shard_map/ppermute | solution.py:54
  42.3 8.5 %collective-permute-start.21 = (bf16[64,512]{1,0:T(8,128)(2,1)S(1)}, bf16[64,512]{1,0:T(8,128)(2,1)S(1)}, u32[]{:S(2)}, u32[]{:S(2)}) collective-permute-start(bf16[64,512]{1,0:T(8,128)(2,1)S(1)} %get-tuple-element.52), channel_id=1, source_target_pairs={{0,20},{4,16},{8,28},{12,24},{16,4},{20,0},{24,12},{28,8},{1,21},{... | collective-permute-start | bytes 196616 | tf_op jit(solution)/shard_map/ppermute | solution.py:54
  43.0 10.4 %collective-permute-start.22 = (bf16[64,512]{1,0:T(8,128)(2,1)S(1)}, bf16[64,512]{1,0:T(8,128)(2,1)S(1)}, u32[]{:S(2)}, u32[]{:S(2)}) collective-permute-start(bf16[64,512]{1,0:T(8,128)(2,1)S(1)} %get-tuple-element.53), channel_id=1, source_target_pairs={{0,24},{4,28},{8,16},{12,20},{16,8},{20,12},{24,0},{28,4},{1,25},{... | collective-permute-start | bytes 196616 | tf_op jit(solution)/shard_map/ppermute | solution.py:54
  43.8 11.3 %collective-permute-start.23 = (bf16[64,512]{1,0:T(8,128)(2,1)S(1)}, bf16[64,512]{1,0:T(8,128)(2,1)S(1)}, u32[]{:S(2)}, u32[]{:S(2)}) collective-permute-start(bf16[64,512]{1,0:T(8,128)(2,1)S(1)} %get-tuple-element.54), channel_id=1, source_target_pairs={{0,28},{4,24},{8,20},{12,16},{16,12},{20,8},{24,4},{28,0},{1,29},{... | collective-permute-start | bytes 196616 | tf_op jit(solution)/shard_map/ppermute | solution.py:54
where the time goes:
time: 56.5 us; the launch traced here: 56.3 us
  starting transfers between devices  26.2 us (46%)
  waiting for transfers between devices  20.8 us (37%)
  Pallas kernels  9.16 us (16%)
    ppermute x22, waiting for transfers between devices, rounds(): out[k] = lax.ppermute(x[k], axis, [(i, to(i, k, n)) for i in range(n)])  19.8 us
    ppermute x22, starting transfers between devices, rounds(): out[k] = lax.ppermute(x[k], axis, [(i, to(i, k, n)) for i in range(n)])  18.6 us
    ppermute x2, starting transfers between devices, gather(): lax.ppermute(out, 'row', [(i, across(i, n)) for i in range(n)])  7.65 us
    pallas_call x2, Pallas kernels, merge(): pl.pallas_call(functools.partial(merge_kernel, n, slots, messages), out_s...  3.53 us
    pallas_call x1, Pallas kernels, on_device(): pl.pallas_call(functools.partial(attend_kernel, n, n_col), out_shape=[sha...  1.83 us
    pallas_call x2, Pallas kernels, project(): pl.pallas_call(functools.partial(project_kernel, m, rows, not tags, skip)...  1.34 us
    pallas_call x1, Pallas kernels, on_device(): pl.pallas_call(functools.partial(return_kernel, n), out_shape=shape(toks,...  1.23 us
  transfers between devices with their start and end apart: 24, of which 9 were waited for; matrix products, arithmetic and copies ran while one was open for 0% of the time, Pallas kernels for 8%

commit v1 on v0

--- a/solution.py
+++ b/solution.py
@@ -66,7 +66,8 @@
 PARTS = (FIRST, SECOND)
 MESSAGES = (
     ((True, *FIRST),),
-    ((True, *SECOND), (False, *FIRST)),
+    ((True, *SECOND),),
+    ((False, *FIRST),),
     ((False, *SECOND),),
 )
 
@@ -179,7 +180,7 @@
             out_ref[s * (size // OWN) + h : s * (size // OWN) + h + rows, :] = pick[s]
 
 
-def project_kernel(m, rows, tagged, skip, wq_ref, wk_ref, wv_ref, cross_ref, *refs):
+def project_kernel(m, rows, tagged, wq_ref, wk_ref, wv_ref, cross_ref, *refs):
     blocks, refs = refs[:m], refs[m:]
     if tagged:
         q_ref, kv_ref, tag_ref, x_ref = refs
@@ -189,7 +190,7 @@
     size = pieces * rows
     if tagged:
         for k in range(m):
-            tag_ref[k] = blocks[k][skip + size : skip + size + TAG, :]
+            tag_ref[k] = blocks[k][size : size + TAG, :]
             tag_ref[m + k] = jnp.broadcast_to(
                 cross_ref[OWN * size + k : OWN * size + k + 1, :], (TAG, LANES)
             )
@@ -197,7 +198,7 @@
     for h in range(pieces):
         pick = [jnp.zeros((rows, LANES), jnp.bfloat16)] * OWN
         for k in range(m):
-            block = blocks[k][skip + h * rows : skip + (h + 1) * rows, :]
+            block = blocks[k][h * rows : (h + 1) * rows, :]
             pick = [jnp.where(masks[k][s], block, pick[s]) for s in range(OWN)]
         for s in range(OWN):
             other = cross_ref[s * size + h * rows : s * size + (h + 1) * rows, :]
@@ -361,10 +362,10 @@
         )(*blocks, *known)
         return out, lax.ppermute(out, "row", [(i, across(i, n)) for i in range(n)])
 
-    def project(c, skip, cross, blocks, *tags):
+    def project(c, cross, blocks, *tags):
         rows = PARTS[c][1]
         out = pl.pallas_call(
-            functools.partial(project_kernel, m, rows, not tags, skip),
+            functools.partial(project_kernel, m, rows, not tags),
             out_shape=[shape(OWN * rows, heads), shape(OWN * rows, 2 * heads)]
             + [shape(n, TAG, LANES)] * (not tags),
             in_specs=[VMEM] * (4 + m + len(tags)),
@@ -378,13 +379,14 @@
 
     (far0,) = merge(0)
     far0 = rounds(far0, "row", n, inner)
-    far1, home1 = merge(1, 2)
+    far1, own0, own1 = merge(1, 2, 3)
     far1 = rounds(far1, "row", n, inner)
     known, cross0 = gather(0, far0)
-    home1 = rounds(home1, "row", n, inner)
+    own0 = rounds(own0, "row", n, inner)
+    own1 = rounds(own1, "row", n, inner)
     _, cross1 = gather(1, far1, known)
-    (q0, _, tags), kv0 = project(0, SECOND[1] * pieces, cross0, far1)
-    (q1, _), kv1 = project(1, 0, cross1, home1, tags)
+    (q0, _, tags), kv0 = project(0, cross0, own0)
+    (q1, _), kv1 = project(1, cross1, own1, tags)
     qs, kvs = [q0, q1], kv0 + kv1
     spread = pl.pallas_call(
         functools.partial(spread_kernel, n, slots),

time: 56.5 us -> 59.8 us (1.058)
  the two profiles are of different devices: /device:TPU:13 before, /device:TPU:0 now
where the time goes in v1:
time: 59.8 us; the launch traced here: 59 us
  starting transfers between devices  31.3 us (52%)
  waiting for transfers between devices  18.4 us (31%)
  Pallas kernels  9.16 us (15%)
    ppermute x25, starting transfers between devices, rounds(): out[k] = lax.ppermute(x[k], axis, [(i, to(i, k, n)) for i in range(n)])  28.3 us
    ppermute x25, waiting for transfers between devices, rounds(): out[k] = lax.ppermute(x[k], axis, [(i, to(i, k, n)) for i in range(n)])  17.3 us
    pallas_call x2, Pallas kernels, merge(): pl.pallas_call(functools.partial(merge_kernel, n, slots, messages), out_s...  3.53 us
    ppermute x2, starting transfers between devices, gather(): lax.ppermute(out, 'row', [(i, across(i, n)) for i in range(n)])  2.98 us
    pallas_call x1, Pallas kernels, on_device(): pl.pallas_call(functools.partial(attend_kernel, n, n_col), out_shape=[sha...  1.84 us
    pallas_call x2, Pallas kernels, project(): pl.pallas_call(functools.partial(project_kernel, m, rows, not tags), out_...  1.34 us
    pallas_call x1, Pallas kernels, on_device(): pl.pallas_call(functools.partial(return_kernel, n), out_shape=shape(toks,...  1.23 us
  transfers between devices with their start and end apart: 27, of which 9 were waited for; matrix products, arithmetic and copies ran while one was open for 0% of the time, Pallas kernels for 7%

profile of v1, /device:TPU:0, one launch (start us, length us, event | category | flops | bytes accessed | tf_op | source)
XLA Modules:
  0.0 59.0 jit_solution(4686413823260696882)
XLA Ops:
  0.0 1.6 %merge.2 = (bf16[264,128]{1,0:T(8,128)(2,1)S(1)}, bf16[264,128]{1,0:T(8,128)(2,1)S(1)}, bf16[264,128]{1,0:T(8,128)(2,1)S(1)}, bf16[264,128]{1,0:T(8,128)(2,1)S(1)}) custom-call(bf16[512,1024]{1,0:T(8,128)(2,1)} %tok_hbm.3, s32[1,512]{1,0:T(1,128)} %bitcast.1, s32[1,8]{1,0:T(1,128)} %owner_hbm.3), custom_call_target="tpu_custom_call" | custom-call | flops 1600000000 | bytes 4000000 | tf_op jit(solution)/shard_map/merge/pallas_call | solution.py:335
  1.6 0.6 collective-permute-start
  2.1 2.6 %collective-permute-start.1 = (bf16[264,128]{1,0:T(8,128)(2,1)S(1)}, bf16[264,128]{1,0:T(8,128)(2,1)S(1)}, u32[]{:S(2)}, u32[]{:S(2)}) collective-permute-start(bf16[264,128]{1,0:T(8,128)(2,1)S(1)} %get-tuple-element.36), channel_id=1, source_target_pairs={{0,8},{4,12},{8,0},{12,4},{16,24},{20,28},{24,16},{28,20},{1,9},{5... | collective-permute-start | bytes 202760 | tf_op jit(solution)/shard_map/ppermute | solution.py:54
  4.8 2.0 %merge.3 = (bf16[256,128]{1,0:T(8,128)(2,1)S(1)}, bf16[256,128]{1,0:T(8,128)(2,1)S(1)}, bf16[256,128]{1,0:T(8,128)(2,1)S(1)}, bf16[256,128]{1,0:T(8,128)(2,1)S(1...) custom-call(bf16[512,1024]{1,0:T(8,128)(2,1)} %tok_hbm.3, ...), custom_call_target="tpu_custom_call" | custom-call | flops 1600000000 | bytes 4000000 | tf_op jit(solution)/shard_map/merge/pallas_call | solution.py:335
  7.0 1.9 %collective-permute-start.8 = (bf16[256,128]{1,0:T(8,128)(2,1)S(1)}, bf16[256,128]{1,0:T(8,128)(2,1)S(1)}, u32[]{:S(2)}, u32[]{:S(2)}) collective-permute-start(bf16[256,128]{1,0:T(8,128)(2,1)S(1)} %get-tuple-element.46), channel_id=1, source_target_pairs={{0,8},{4,12},{8,0},{12,4},{16,24},{20,28},{24,16},{28,20},{1,9},{5... | collective-permute-start | bytes 196616 | tf_op jit(solution)/shard_map/ppermute | solution.py:54
  9.1 2.6 %collective-permute-start.3 = (bf16[520,128]{1,0:T(8,128)(2,1)S(1)}, bf16[520,128]{1,0:T(8,128)(2,1)S(1)}, u32[]{:S(2)}, u32[]{:S(2)}) collective-permute-start(bf16[520,128]{1,0:T(8,128)(2,1)S(1)} %gather.2.refs_4_), channel_id=1, source_target_pairs={{0,16},{4,20},{8,24},{12,28},{16,0},{20,4},{24,8},{28,12},{1,17},{... | collective-permute-start | bytes 399368 | tf_op jit(solution)/shard_map/ppermute | solution.py:363
  12.0 1.6 %collective-permute-start.5 = (bf16[264,128]{1,0:T(8,128)(2,1)S(1)}, bf16[264,128]{1,0:T(8,128)(2,1)S(1)}, u32[]{:S(2)}, u32[]{:S(2)}) collective-permute-start(bf16[264,128]{1,0:T(8,128)(2,1)S(1)} %get-tuple-element.40), channel_id=1, source_target_pairs={{0,8},{4,12},{8,0},{12,4},{16,24},{20,28},{24,16},{28,20},{1,9},{5... | collective-permute-start | bytes 202760 | tf_op jit(solution)/shard_map/ppermute | solution.py:54
  13.6 2.0 %collective-permute-done.9.refs_3_ = bf16[256,128]{1,0:T(8,128)(2,1)S(1)} collective-permute-done((bf16[256,128]{1,0:T(8,128)(2,1)S(1)}, bf16[256,128]{1,0:T(8,128)(2,1)S(1)}, u32[]{:S(2)}, u32[]{:S(2)}) %collective-permute-start.9) | collective-permute-done | bytes 65568 | tf_op jit(solution)/shard_map/ppermute | solution.py:54
  16.3 0.8 %collective-permute-done.5.refs_2_ = bf16[264,128]{1,0:T(8,128)(2,1)S(1)} collective-permute-done((bf16[264,128]{1,0:T(8,128)(2,1)S(1)}, bf16[264,128]{1,0:T(8,128)(2,1)S(1)}, u32[]{:S(2)}, u32[]{:S(2)}) %collective-permute-start.5) | collective-permute-done | bytes 67616 | tf_op jit(solution)/shard_map/ppermute | solution.py:54
  17.2 2.5 %collective-permute-start.12 = (bf16[256,128]{1,0:T(8,128)(2,1)S(1)}, bf16[256,128]{1,0:T(8,128)(2,1)S(1)}, u32[]{:S(2)}, u32[]{:S(2)}) collective-permute-start(bf16[256,128]{1,0:T(8,128)(2,1)S(1)} %get-tuple-element.50), channel_id=1, source_target_pairs={{0,8},{4,12},{8,0},{12,4},{16,24},{20,28},{24,16},{28,20},{1,9},{5... | collective-permute-start | bytes 196616 | tf_op jit(solution)/shard_map/ppermute | solution.py:54
  19.6 0.9 %collective-permute-start.13 = (bf16[256,128]{1,0:T(8,128)(2,1)S(1)}, bf16[256,128]{1,0:T(8,128)(2,1)S(1)}, u32[]{:S(2)}, u32[]{:S(2)}) collective-permute-start(bf16[256,128]{1,0:T(8,128)(2,1)S(1)} %get-tuple-element.51), channel_id=1, source_target_pairs={{0,12},{4,8},{8,4},{12,0},{16,28},{20,24},{24,20},{28,16},{1,13},{... | collective-permute-start | bytes 196616 | tf_op jit(solution)/shard_map/ppermute | solution.py:54
  20.5 0.7 %project.2 = (bf16[64,512]{1,0:T(8,128)(2,1)S(1)}, bf16[64,1024]{1,0:T(8,128)(2,1)S(1)}, bf16[8,8,128]{2,1,0:T(8,128)(2,1)S(1)}) custom-call(bf16[1024,512]{1,0:T(8,128)(2,1)S(1)} %copy-done, bf16[1024,512]{1,0:T(8,128)(2,1)S(1)} %copy-done.1, bf16[1024,512]{1,0:T(8,128)(2,1)S(1)} %copy-done.2, bf16[520,128]{1,0:T(8,128)(2,1)S(1)} %collective-permute-done.3.cross_ref, ...), custom_call_target="tpu_custom_call" | custom-call | flops 800000000 | bytes 2000000 | tf_op jit(solution)/shard_map/project/pallas_call | solution.py:367
  21.2 1.6 %collective-permute-done.12.refs_2_ = bf16[256,128]{1,0:T(8,128)(2,1)S(1)} collective-permute-done((bf16[256,128]{1,0:T(8,128)(2,1)S(1)}, bf16[256,128]{1,0:T(8,128)(2,1)S(1)}, u32[]{:S(2)}, u32[]{:S(2)}) %collective-permute-start.12) | collective-permute-done | bytes 65568 | tf_op jit(solution)/shard_map/ppermute | solution.py:54
  22.8 1.2 %collective-permute-done.13.refs_3_ = bf16[256,128]{1,0:T(8,128)(2,1)S(1)} collective-permute-done((bf16[256,128]{1,0:T(8,128)(2,1)S(1)}, bf16[256,128]{1,0:T(8,128)(2,1)S(1)}, u32[]{:S(2)}, u32[]{:S(2)}) %collective-permute-start.13) | collective-permute-done | bytes 65568 | tf_op jit(solution)/shard_map/ppermute | solution.py:54
  24.0 1.0 %collective-permute-done.10.cross_ref = bf16[512,128]{1,0:T(8,128)(2,1)S(1)} collective-permute-done((bf16[512,128]{1,0:T(8,128)(2,1)S(1)}, bf16[512,128]{1,0:T(8,128)(2,1)S(1)}, u32[]{:S(2)}, u32[]{:S(2)}) %collective-permute-start.10) | collective-permute-done | bytes 131104 | tf_op jit(solution)/shard_map/ppermute | solution.py:363
  25.1 0.7 %project.3 = (bf16[64,512]{1,0:T(8,128)(2,1)S(1)}, bf16[64,1024]{1,0:T(8,128)(2,1)S(1)}) custom-call(bf16[1024,512]{1,0:T(8,128)(2,1)S(1)} %copy-done, bf16[1024,512]{1,0:T(8,128)(2,1)S(1)} %copy-done.1, bf16[1024,512]{1,0:T(8,128)(2,1)S(1)} %copy-done.2, bf16[512,128]{1,0:T(8,128)(2,1)S(1)} %collective-permute-done.10.cross_ref, ...), custom_call_target="tpu_custom_call" | custom-call | flops 800000000 | bytes 2000000 | tf_op jit(solution)/shard_map/project/pallas_call | solution.py:367
  25.7 1.5 %collective-permute-start.17 = (bf16[64,1024]{1,0:T(8,128)(2,1)S(1)}, bf16[64,1024]{1,0:T(8,128)(2,1)S(1)}, u32[]{:S(2)}, u32[]{:S(2)}) collective-permute-start(bf16[64,1024]{1,0:T(8,128)(2,1)S(1)} %get-tuple-element.54.refs_6_), channel_id=1, source_target_pairs={{0,1},{1,0},{2,3},{3,2},{4,5},{5,4},{6,7},{7,6},{8,9},{9,8},{10,11... | collective-permute-start | bytes 393224 | tf_op jit(solution)/shard_map/ppermute | solution.py:54
  27.2 1.5 %collective-permute-start.18 = (bf16[64,1024]{1,0:T(8,128)(2,1)S(1)}, bf16[64,1024]{1,0:T(8,128)(2,1)S(1)}, u32[]{:S(2)}, u32[]{:S(2)}) collective-permute-start(bf16[64,1024]{1,0:T(8,128)(2,1)S(1)} %get-tuple-element.54.refs_6_), channel_id=1, source_target_pairs={{0,2},{1,3},{2,0},{3,1},{4,6},{5,7},{6,4},{7,5},{8,10},{9,11},{10,... | collective-permute-start | bytes 393224 | tf_op jit(solution)/shard_map/ppermute | solution.py:54
  28.8 0.5 collective-permute-start.19
  29.3 1.4 %collective-permute-start.14 = (bf16[64,1024]{1,0:T(8,128)(2,1)S(1)}, bf16[64,1024]{1,0:T(8,128)(2,1)S(1)}, u32[]{:S(2)}, u32[]{:S(2)}) collective-permute-start(bf16[64,1024]{1,0:T(8,128)(2,1)S(1)} %get-tuple-element.53.refs_2_), channel_id=1, source_target_pairs={{0,1},{1,0},{2,3},{3,2},{4,5},{5,4},{6,7},{7,6},{8,9},{9,8},{10,11... | collective-permute-start | bytes 393224 | tf_op jit(solution)/shard_map/ppermute | solution.py:54
  30.7 1.5 %collective-permute-start.15 = (bf16[64,1024]{1,0:T(8,128)(2,1)S(1)}, bf16[64,1024]{1,0:T(8,128)(2,1)S(1)}, u32[]{:S(2)}, u32[]{:S(2)}) collective-permute-start(bf16[64,1024]{1,0:T(8,128)(2,1)S(1)} %get-tuple-element.53.refs_2_), channel_id=1, source_target_pairs={{0,2},{1,3},{2,0},{3,1},{4,6},{5,7},{6,4},{7,5},{8,10},{9,11},{10,... | collective-permute-start | bytes 393224 | tf_op jit(solution)/shard_map/ppermute | solution.py:54
  32.3 2.3 %collective-permute-start.16 = (bf16[64,1024]{1,0:T(8,128)(2,1)S(1)}, bf16[64,1024]{1,0:T(8,128)(2,1)S(1)}, u32[]{:S(2)}, u32[]{:S(2)}) collective-permute-start(bf16[64,1024]{1,0:T(8,128)(2,1)S(1)} %get-tuple-element.53.refs_2_), channel_id=1, source_target_pairs={{0,3},{1,2},{2,1},{3,0},{4,7},{5,6},{6,5},{7,4},{8,11},{9,10},{10,... | collective-permute-start | bytes 393224 | tf_op jit(solution)/shard_map/ppermute | solution.py:54
  34.6 1.5 %collective-permute-done.18.refs_8_ = bf16[64,1024]{1,0:T(8,128)(2,1)S(1)} collective-permute-done((bf16[64,1024]{1,0:T(8,128)(2,1)S(1)}, bf16[64,1024]{1,0:T(8,128)(2,1)S(1)}, u32[]{:S(2)}, u32[]{:S(2)}) %collective-permute-start.18) | collective-permute-done | bytes 131104 | tf_op jit(solution)/shard_map/ppermute | solution.py:54
  36.1 1.7 %collective-permute-done.14.refs_3_ = bf16[64,1024]{1,0:T(8,128)(2,1)S(1)} collective-permute-done((bf16[64,1024]{1,0:T(8,128)(2,1)S(1)}, bf16[64,1024]{1,0:T(8,128)(2,1)S(1)}, u32[]{:S(2)}, u32[]{:S(2)}) %collective-permute-start.14) | collective-permute-done | bytes 131104 | tf_op jit(solution)/shard_map/ppermute | solution.py:54
  37.8 2.8 %collective-permute-done.15.refs_4_ = bf16[64,1024]{1,0:T(8,128)(2,1)S(1)} collective-permute-done((bf16[64,1024]{1,0:T(8,128)(2,1)S(1)}, bf16[64,1024]{1,0:T(8,128)(2,1)S(1)}, u32[]{:S(2)}, u32[]{:S(2)}) %collective-permute-start.15) | collective-permute-done | bytes 131104 | tf_op jit(solution)/shard_map/ppermute | solution.py:54
  40.6 1.8 %attend.1 = (bf16[64,512]{1,0:T(8,128)(2,1)S(1)}, bf16[64,512]{1,0:T(8,128)(2,1)S(1)}, bf16[64,512]{1,0:T(8,128)(2,1)S(1)}, bf16[64,512]{1,0:T(8,128)(2,1)S(1)},...) custom-call(s32[2,4]{1,0:T(2,128)} %near_ref.1, ...), custom_call_target="tpu_custom_call" | custom-call | flops 2400000000 | bytes 6000000 | tf_op jit(solution)/shard_map/attend/pallas_call | solution.py:400
  42.5 1.4 %collective-permute-start.21 = (bf16[64,512]{1,0:T(8,128)(2,1)S(1)}, bf16[64,512]{1,0:T(8,128)(2,1)S(1)}, u32[]{:S(2)}, u32[]{:S(2)}) collective-permute-start(bf16[64,512]{1,0:T(8,128)(2,1)S(1)} %get-tuple-element.57), channel_id=1, source_target_pairs={{0,8},{4,12},{8,0},{12,4},{16,24},{20,28},{24,16},{28,20},{1,9},{5... | collective-permute-start | bytes 196616 | tf_op jit(solution)/shard_map/ppermute | solution.py:54
  44.4 2.7 %collective-permute-start.23 = (bf16[64,512]{1,0:T(8,128)(2,1)S(1)}, bf16[64,512]{1,0:T(8,128)(2,1)S(1)}, u32[]{:S(2)}, u32[]{:S(2)}) collective-permute-start(bf16[64,512]{1,0:T(8,128)(2,1)S(1)} %get-tuple-element.59), channel_id=1, source_target_pairs={{0,16},{4,20},{8,24},{12,28},{16,0},{20,4},{24,8},{28,12},{1,17},{... | collective-permute-start | bytes 196616 | tf_op jit(solution)/shard_map/ppermute | solution.py:54
  47.1 3.8 %collective-permute-start.25 = (bf16[64,512]{1,0:T(8,128)(2,1)S(1)}, bf16[64,512]{1,0:T(8,128)(2,1)S(1)}, u32[]{:S(2)}, u32[]{:S(2)}) collective-permute-start(bf16[64,512]{1,0:T(8,128)(2,1)S(1)} %get-tuple-element.61), channel_id=1, source_target_pairs={{0,24},{4,28},{8,16},{12,20},{16,8},{20,12},{24,0},{28,4},{1,25},{... | collective-permute-start | bytes 196616 | tf_op jit(solution)/shard_map/ppermute | solution.py:54
  51.0 1.1 %spread.1.spread_ref = bf16[512,512]{1,0:T(8,128)(2,1)S(1)} custom-call(s32[1,512]{1,0:T(1,128)} %bitcast.3, s32[1,8]{1,0:T(1,128)} %owner_hbm.3), custom_call_target="tpu_custom_call" | custom-call | flops 1600000000 | bytes 4000000 | tf_op jit(solution)/shard_map/spread/pallas_call | solution.py:391
  52.2 5.6 %collective-permute-done.24.refs_5_ = bf16[64,512]{1,0:T(8,128)(2,1)S(1)} collective-permute-done((bf16[64,512]{1,0:T(8,128)(2,1)S(1)}, bf16[64,512]{1,0:T(8,128)(2,1)S(1)}, u32[]{:S(2)}, u32[]{:S(2)}) %collective-permute-start.24) | collective-permute-done | bytes 65568 | tf_op jit(solution)/shard_map/ppermute | solution.py:54
  57.8 1.2 %give_back.1 = bf16[512,512]{1,0:T(8,128)(2,1)} custom-call(bf16[512,512]{1,0:T(8,128)(2,1)S(1)} %spread.1.spread_ref, bf16[64,512]{1,0:T(8,128)(2,1)S(1)} %get-tuple-element.55.refs_0_, bf16[64,512]{1,0:T(8,128)(2,1)S(1)} %collective-permute-done.20.refs_1_, bf16[64,512]{1,0:T(8,128)(2,1)S(1)} %collective-permute-done.21.refs_2_, ...), custom_call_target="tpu_custom_call" | custom-call | flops 1600000000 | bytes 4000000 | tf_op jit(solution)/shard_map/give_back/pallas_call | solution.py:414
  (37 shorter events, 2.1 us)
Async XLA Ops:
  1.6 7.4 %collective-permute-start = (bf16[264,128]{1,0:T(8,128)(2,1)S(1)}, bf16[264,128]{1,0:T(8,128)(2,1)S(1)}, u32[]{:S(2)}, u32[]{:S(2)}) collective-permute-start(bf16[264,128]{1,0:T(8,128)(2,1)S(1)} %get-tuple-element.35), channel_id=1, source_target_pairs={{0,4},{4,0},{8,12},{12,8},{16,20},{20,16},{24,28},{28,24},{1,5},{5... | collective-permute-start | bytes 202760 | tf_op jit(solution)/shard_map/ppermute | solution.py:54
  2.1 6.8 %collective-permute-start.1 = (bf16[264,128]{1,0:T(8,128)(2,1)S(1)}, bf16[264,128]{1,0:T(8,128)(2,1)S(1)}, u32[]{:S(2)}, u32[]{:S(2)}) collective-permute-start(bf16[264,128]{1,0:T(8,128)(2,1)S(1)} %get-tuple-element.36), channel_id=1, source_target_pairs={{0,8},{4,12},{8,0},{12,4},{16,24},{20,28},{24,16},{28,20},{1,9},{5... | collective-permute-start | bytes 202760 | tf_op jit(solution)/shard_map/ppermute | solution.py:54
  4.8 4.2 %collective-permute-start.2 = (bf16[264,128]{1,0:T(8,128)(2,1)S(1)}, bf16[264,128]{1,0:T(8,128)(2,1)S(1)}, u32[]{:S(2)}, u32[]{:S(2)}) collective-permute-start(bf16[264,128]{1,0:T(8,128)(2,1)S(1)} %get-tuple-element.37), channel_id=1, source_target_pairs={{0,12},{4,8},{8,4},{12,0},{16,28},{20,24},{24,20},{28,16},{1,13},{... | collective-permute-start | bytes 202760 | tf_op jit(solution)/shard_map/ppermute | solution.py:54
  4.8 15.7 %copy-start.2 = (bf16[1024,512]{1,0:T(8,128)(2,1)S(1)}, bf16[1024,512]{1,0:T(8,128)(2,1)}, u32[]{:S(2)}) copy-start(bf16[1024,512]{1,0:T(8,128)(2,1)} %wv_ref.3) | copy-start | bytes 3145732
  6.8 5.2 %collective-permute-start.7 = (bf16[256,128]{1,0:T(8,128)(2,1)S(1)}, bf16[256,128]{1,0:T(8,128)(2,1)S(1)}, u32[]{:S(2)}, u32[]{:S(2)}) collective-permute-start(bf16[256,128]{1,0:T(8,128)(2,1)S(1)} %get-tuple-element.45), channel_id=1, source_target_pairs={{0,4},{4,0},{8,12},{12,8},{16,20},{20,16},{24,28},{28,24},{1,5},{5... | collective-permute-start | bytes 196616 | tf_op jit(solution)/shard_map/ppermute | solution.py:54
  7.0 6.6 %collective-permute-start.8 = (bf16[256,128]{1,0:T(8,128)(2,1)S(1)}, bf16[256,128]{1,0:T(8,128)(2,1)S(1)}, u32[]{:S(2)}, u32[]{:S(2)}) collective-permute-start(bf16[256,128]{1,0:T(8,128)(2,1)S(1)} %get-tuple-element.46), channel_id=1, source_target_pairs={{0,8},{4,12},{8,0},{12,4},{16,24},{20,28},{24,16},{28,20},{1,9},{5... | collective-permute-start | bytes 196616 | tf_op jit(solution)/shard_map/ppermute | solution.py:54
  9.0 6.7 %collective-permute-start.9 = (bf16[256,128]{1,0:T(8,128)(2,1)S(1)}, bf16[256,128]{1,0:T(8,128)(2,1)S(1)}, u32[]{:S(2)}, u32[]{:S(2)}) collective-permute-start(bf16[256,128]{1,0:T(8,128)(2,1)S(1)} %get-tuple-element.47), channel_id=1, source_target_pairs={{0,12},{4,8},{8,4},{12,0},{16,28},{20,24},{24,20},{28,16},{1,13},{... | collective-permute-start | bytes 196616 | tf_op jit(solution)/shard_map/ppermute | solution.py:54
  9.0 11.5 %copy-start.1 = (bf16[1024,512]{1,0:T(8,128)(2,1)S(1)}, bf16[1024,512]{1,0:T(8,128)(2,1)}, u32[]{:S(2)}) copy-start(bf16[1024,512]{1,0:T(8,128)(2,1)} %wk_ref.3) | copy-start | bytes 3145732
  9.1 11.5 %copy-start = (bf16[1024,512]{1,0:T(8,128)(2,1)S(1)}, bf16[1024,512]{1,0:T(8,128)(2,1)}, u32[]{:S(2)}) copy-start(bf16[1024,512]{1,0:T(8,128)(2,1)} %wq_ref.3) | copy-start | bytes 3145732
  9.1 11.4 %collective-permute-start.3 = (bf16[520,128]{1,0:T(8,128)(2,1)S(1)}, bf16[520,128]{1,0:T(8,128)(2,1)S(1)}, u32[]{:S(2)}, u32[]{:S(2)}) collective-permute-start(bf16[520,128]{1,0:T(8,128)(2,1)S(1)} %gather.2.refs_4_), channel_id=1, source_target_pairs={{0,16},{4,20},{8,24},{12,28},{16,0},{20,4},{24,8},{28,12},{1,17},{... | collective-permute-start | bytes 399368 | tf_op jit(solution)/shard_map/ppermute | solution.py:363
  11.7 4.3 %collective-permute-start.4 = (bf16[264,128]{1,0:T(8,128)(2,1)S(1)}, bf16[264,128]{1,0:T(8,128)(2,1)S(1)}, u32[]{:S(2)}, u32[]{:S(2)}) collective-permute-start(bf16[264,128]{1,0:T(8,128)(2,1)S(1)} %get-tuple-element.39), channel_id=1, source_target_pairs={{0,4},{4,0},{8,12},{12,8},{16,20},{20,16},{24,28},{28,24},{1,5},{5... | collective-permute-start | bytes 202760 | tf_op jit(solution)/shard_map/ppermute | solution.py:54
  12.0 5.2 %collective-permute-start.5 = (bf16[264,128]{1,0:T(8,128)(2,1)S(1)}, bf16[264,128]{1,0:T(8,128)(2,1)S(1)}, u32[]{:S(2)}, u32[]{:S(2)}) collective-permute-start(bf16[264,128]{1,0:T(8,128)(2,1)S(1)} %get-tuple-element.40), channel_id=1, source_target_pairs={{0,8},{4,12},{8,0},{12,4},{16,24},{20,28},{24,16},{28,20},{1,9},{5... | collective-permute-start | bytes 202760 | tf_op jit(solution)/shard_map/ppermute | solution.py:54
  13.6 6.1 %collective-permute-start.6 = (bf16[264,128]{1,0:T(8,128)(2,1)S(1)}, bf16[264,128]{1,0:T(8,128)(2,1)S(1)}, u32[]{:S(2)}, u32[]{:S(2)}) collective-permute-start(bf16[264,128]{1,0:T(8,128)(2,1)S(1)} %get-tuple-element.41), channel_id=1, source_target_pairs={{0,12},{4,8},{8,4},{12,0},{16,28},{20,24},{24,20},{28,16},{1,13},{... | collective-permute-start | bytes 202760 | tf_op jit(solution)/shard_map/ppermute | solution.py:54
  15.7 9.4 %collective-permute-start.10 = (bf16[512,128]{1,0:T(8,128)(2,1)S(1)}, bf16[512,128]{1,0:T(8,128)(2,1)S(1)}, u32[]{:S(2)}, u32[]{:S(2)}) collective-permute-start(bf16[512,128]{1,0:T(8,128)(2,1)S(1)} %gather.3), channel_id=1, source_target_pairs={{0,16},{4,20},{8,24},{12,28},{16,0},{20,4},{24,8},{28,12},{1,17},{... | collective-permute-start | bytes 393224 | tf_op jit(solution)/shard_map/ppermute | solution.py:363
  16.0 5.2 %collective-permute-start.11 = (bf16[256,128]{1,0:T(8,128)(2,1)S(1)}, bf16[256,128]{1,0:T(8,128)(2,1)S(1)}, u32[]{:S(2)}, u32[]{:S(2)}) collective-permute-start(bf16[256,128]{1,0:T(8,128)(2,1)S(1)} %get-tuple-element.49), channel_id=1, source_target_pairs={{0,4},{4,0},{8,12},{12,8},{16,20},{20,16},{24,28},{28,24},{1,5},{5... | collective-permute-start | bytes 196616 | tf_op jit(solution)/shard_map/ppermute | solution.py:54
  17.2 5.7 %collective-permute-start.12 = (bf16[256,128]{1,0:T(8,128)(2,1)S(1)}, bf16[256,128]{1,0:T(8,128)(2,1)S(1)}, u32[]{:S(2)}, u32[]{:S(2)}) collective-permute-start(bf16[256,128]{1,0:T(8,128)(2,1)S(1)} %get-tuple-element.50), channel_id=1, source_target_pairs={{0,8},{4,12},{8,0},{12,4},{16,24},{20,28},{24,16},{28,20},{1,9},{5... | collective-permute-start | bytes 196616 | tf_op jit(solution)/shard_map/ppermute | solution.py:54
  19.6 4.4 %collective-permute-start.13 = (bf16[256,128]{1,0:T(8,128)(2,1)S(1)}, bf16[256,128]{1,0:T(8,128)(2,1)S(1)}, u32[]{:S(2)}, u32[]{:S(2)}) collective-permute-start(bf16[256,128]{1,0:T(8,128)(2,1)S(1)} %get-tuple-element.51), channel_id=1, source_target_pairs={{0,12},{4,8},{8,4},{12,0},{16,28},{20,24},{24,20},{28,16},{1,13},{... | collective-permute-start | bytes 196616 | tf_op jit(solution)/shard_map/ppermute | solution.py:54
  25.7 6.5 %collective-permute-start.17 = (bf16[64,1024]{1,0:T(8,128)(2,1)S(1)}, bf16[64,1024]{1,0:T(8,128)(2,1)S(1)}, u32[]{:S(2)}, u32[]{:S(2)}) collective-permute-start(bf16[64,1024]{1,0:T(8,128)(2,1)S(1)} %get-tuple-element.54.refs_6_), channel_id=1, source_target_pairs={{0,1},{1,0},{2,3},{3,2},{4,5},{5,4},{6,7},{7,6},{8,9},{9,8},{10,11... | collective-permute-start | bytes 393224 | tf_op jit(solution)/shard_map/ppermute | solution.py:54
  27.2 8.8 %collective-permute-start.18 = (bf16[64,1024]{1,0:T(8,128)(2,1)S(1)}, bf16[64,1024]{1,0:T(8,128)(2,1)S(1)}, u32[]{:S(2)}, u32[]{:S(2)}) collective-permute-start(bf16[64,1024]{1,0:T(8,128)(2,1)S(1)} %get-tuple-element.54.refs_6_), channel_id=1, source_target_pairs={{0,2},{1,3},{2,0},{3,1},{4,6},{5,7},{6,4},{7,5},{8,10},{9,11},{10,... | collective-permute-start | bytes 393224 | tf_op jit(solution)/shard_map/ppermute | solution.py:54
  28.8 7.3 %collective-permute-start.19 = (bf16[64,1024]{1,0:T(8,128)(2,1)S(1)}, bf16[64,1024]{1,0:T(8,128)(2,1)S(1)}, u32[]{:S(2)}, u32[]{:S(2)}) collective-permute-start(bf16[64,1024]{1,0:T(8,128)(2,1)S(1)} %get-tuple-element.54.refs_6_), channel_id=1, source_target_pairs={{0,3},{1,2},{2,1},{3,0},{4,7},{5,6},{6,5},{7,4},{8,11},{9,10},{10,... | collective-permute-start | bytes 393224 | tf_op jit(solution)/shard_map/ppermute | solution.py:54
  29.3 8.5 %collective-permute-start.14 = (bf16[64,1024]{1,0:T(8,128)(2,1)S(1)}, bf16[64,1024]{1,0:T(8,128)(2,1)S(1)}, u32[]{:S(2)}, u32[]{:S(2)}) collective-permute-start(bf16[64,1024]{1,0:T(8,128)(2,1)S(1)} %get-tuple-element.53.refs_2_), channel_id=1, source_target_pairs={{0,1},{1,0},{2,3},{3,2},{4,5},{5,4},{6,7},{7,6},{8,9},{9,8},{10,11... | collective-permute-start | bytes 393224 | tf_op jit(solution)/shard_map/ppermute | solution.py:54
  30.7 9.9 %collective-permute-start.15 = (bf16[64,1024]{1,0:T(8,128)(2,1)S(1)}, bf16[64,1024]{1,0:T(8,128)(2,1)S(1)}, u32[]{:S(2)}, u32[]{:S(2)}) collective-permute-start(bf16[64,1024]{1,0:T(8,128)(2,1)S(1)} %get-tuple-element.53.refs_2_), channel_id=1, source_target_pairs={{0,2},{1,3},{2,0},{3,1},{4,6},{5,7},{6,4},{7,5},{8,10},{9,11},{10,... | collective-permute-start | bytes 393224 | tf_op jit(solution)/shard_map/ppermute | solution.py:54
  32.3 8.4 %collective-permute-start.16 = (bf16[64,1024]{1,0:T(8,128)(2,1)S(1)}, bf16[64,1024]{1,0:T(8,128)(2,1)S(1)}, u32[]{:S(2)}, u32[]{:S(2)}) collective-permute-start(bf16[64,1024]{1,0:T(8,128)(2,1)S(1)} %get-tuple-element.53.refs_2_), channel_id=1, source_target_pairs={{0,3},{1,2},{2,1},{3,0},{4,7},{5,6},{6,5},{7,4},{8,11},{9,10},{10,... | collective-permute-start | bytes 393224 | tf_op jit(solution)/shard_map/ppermute | solution.py:54
  42.5 4.7 %collective-permute-start.20 = (bf16[64,512]{1,0:T(8,128)(2,1)S(1)}, bf16[64,512]{1,0:T(8,128)(2,1)S(1)}, u32[]{:S(2)}, u32[]{:S(2)}) collective-permute-start(bf16[64,512]{1,0:T(8,128)(2,1)S(1)} %get-tuple-element.56), channel_id=1, source_target_pairs={{0,4},{4,0},{8,12},{12,8},{16,20},{20,16},{24,28},{28,24},{1,5},{5... | collective-permute-start | bytes 196616 | tf_op jit(solution)/shard_map/ppermute | solution.py:54
  42.5 8.4 %collective-permute-start.21 = (bf16[64,512]{1,0:T(8,128)(2,1)S(1)}, bf16[64,512]{1,0:T(8,128)(2,1)S(1)}, u32[]{:S(2)}, u32[]{:S(2)}) collective-permute-start(bf16[64,512]{1,0:T(8,128)(2,1)S(1)} %get-tuple-element.57), channel_id=1, source_target_pairs={{0,8},{4,12},{8,0},{12,4},{16,24},{20,28},{24,16},{28,20},{1,9},{5... | collective-permute-start | bytes 196616 | tf_op jit(solution)/shard_map/ppermute | solution.py:54
  43.9 8.3 %collective-permute-start.22 = (bf16[64,512]{1,0:T(8,128)(2,1)S(1)}, bf16[64,512]{1,0:T(8,128)(2,1)S(1)}, u32[]{:S(2)}, u32[]{:S(2)}) collective-permute-start(bf16[64,512]{1,0:T(8,128)(2,1)S(1)} %get-tuple-element.58), channel_id=1, source_target_pairs={{0,12},{4,8},{8,4},{12,0},{16,28},{20,24},{24,20},{28,16},{1,13},{... | collective-permute-start | bytes 196616 | tf_op jit(solution)/shard_map/ppermute | solution.py:54
  44.4 7.8 %collective-permute-start.23 = (bf16[64,512]{1,0:T(8,128)(2,1)S(1)}, bf16[64,512]{1,0:T(8,128)(2,1)S(1)}, u32[]{:S(2)}, u32[]{:S(2)}) collective-permute-start(bf16[64,512]{1,0:T(8,128)(2,1)S(1)} %get-tuple-element.59), channel_id=1, source_target_pairs={{0,16},{4,20},{8,24},{12,28},{16,0},{20,4},{24,8},{28,12},{1,17},{... | collective-permute-start | bytes 196616 | tf_op jit(solution)/shard_map/ppermute | solution.py:54
  47.1 10.6 %collective-permute-start.24 = (bf16[64,512]{1,0:T(8,128)(2,1)S(1)}, bf16[64,512]{1,0:T(8,128)(2,1)S(1)}, u32[]{:S(2)}, u32[]{:S(2)}) collective-permute-start(bf16[64,512]{1,0:T(8,128)(2,1)S(1)} %get-tuple-element.60), channel_id=1, source_target_pairs={{0,20},{4,16},{8,28},{12,24},{16,4},{20,0},{24,12},{28,8},{1,21},{... | collective-permute-start | bytes 196616 | tf_op jit(solution)/shard_map/ppermute | solution.py:54
  47.1 10.6 %collective-permute-start.25 = (bf16[64,512]{1,0:T(8,128)(2,1)S(1)}, bf16[64,512]{1,0:T(8,128)(2,1)S(1)}, u32[]{:S(2)}, u32[]{:S(2)}) collective-permute-start(bf16[64,512]{1,0:T(8,128)(2,1)S(1)} %get-tuple-element.61), channel_id=1, source_target_pairs={{0,24},{4,28},{8,16},{12,20},{16,8},{20,12},{24,0},{28,4},{1,25},{... | collective-permute-start | bytes 196616 | tf_op jit(solution)/shard_map/ppermute | solution.py:54
  50.9 6.8 %collective-permute-start.26 = (bf16[64,512]{1,0:T(8,128)(2,1)S(1)}, bf16[64,512]{1,0:T(8,128)(2,1)S(1)}, u32[]{:S(2)}, u32[]{:S(2)}) collective-permute-start(bf16[64,512]{1,0:T(8,128)(2,1)S(1)} %get-tuple-element.62), channel_id=1, source_target_pairs={{0,28},{4,24},{8,20},{12,16},{16,12},{20,8},{24,4},{28,0},{1,29},{... | collective-permute-start | bytes 196616 | tf_op jit(solution)/shard_map/ppermute | solution.py:54
